TPU v7x, 256 devices: a whole 4x4x8 slice. The times are simulated.
256 devices in a mesh: leaf: 16 (over y, x), col: 16 (over z, core).
Axes of the slice: x: 4, y: 4, z: 8, core: 2. Of those that a mesh axis runs over, the one named last changes fastest.
Arguments:
- right_sides: bfloat16 [16, 2, 1792, 128], P('leaf', None, 'col'), may hold values from -6 to 6
- leaf_inverse: bfloat16 [16, 1792, 1792], P('leaf', 'col'), as said below
- upper_inverse: bfloat16 [16, 1792, 1792], P('leaf', 'col'), as said below
- leaf_update: bfloat16 [16, 4, 1792, 512], P('leaf', None, 'col'), may hold values from -0.0625 to 0.0625
- upper_update: bfloat16 [16, 4, 1792, 512], P('leaf', None, 'col'), may hold values from -0.0625 to 0.0625
- live_rows: int32 [16, 2], P('leaf'), may hold values from 896 to 1792, as said below
- tile_map: int32 [16, 2, 4, 512], P('leaf'), may hold values from 0 to 1791, as said below
Outputs:
- solution: bfloat16 [16, 2, 1792, 128], P('leaf', None, 'col')
Inputs may be any that keep to these rules, and one draw needn't show every extreme that they name: `leaf_inverse`: zero above the diagonal, nonzero on it. `upper_inverse`: zero above the diagonal, nonzero on it. `live_rows`: one supernode has all 1792 rows live and one has 896. `tile_map`: the rows of one tile are distinct and increasing.
All inputs are finite; a program needn't handle non-finite values.
Results may differ from a plain program's by a relative error of at most 0.0075.
Values may be sent and summed in bfloat16 or wider, within the bound.
No kernel may reach another device: no remote copies, remote signals or barrier semaphores. Data moves between devices by JAX's collectives and lax.ppermute only.
A program may use at most 64 MiB of HBM per device.

v0:
```python
import jax
import jax.numpy as jnp
from jax import lax
from jax.sharding import PartitionSpec as P


def forward_solve(inverse_rows, residual, row_mask, active):
    shares = (residual * row_mask).astype(jnp.bfloat16)
    empty = jnp.zeros((inverse_rows.shape[0], residual.shape[1]), jnp.float32)
    shard_rows = lax.all_gather(shares, "col", axis=0, tiled=True)
    solved = lax.cond(
        active,
        lambda: jnp.dot(inverse_rows, shard_rows, preferred_element_type=jnp.float32),
        lambda: empty,
    )
    return (solved * row_mask).astype(jnp.bfloat16)


def tile_terms(update_cols, solved, active):

    def tile_compute():
        return jnp.einsum("srt,rn->stn", update_cols, solved, preferred_element_type=jnp.float32)

    def tile_nothing():
        return jnp.zeros((update_cols.shape[0], update_cols.shape[2], solved.shape[1]), jnp.float32)

    local_terms = lax.cond(active, tile_compute, tile_nothing)
    return lax.psum(local_terms, "col")


def spread(summed, tile_rows, first_row, rows_dev):
    local_rows = tile_rows - first_row
    inside = (local_rows >= 0) & (local_rows < rows_dev)
    target = jnp.where(inside, local_rows, rows_dev)

    def one_slot(values, where_to):
        return (
            jnp.zeros((rows_dev, values.shape[1]), jnp.float32)
            .at[where_to]
            .add(values, mode="drop")
        )

    return jax.vmap(one_slot)(summed, target)


def pick_rows(fetched, tile_rows, first_row, rows_dev):
    local_rows = tile_rows - first_row
    inside = (local_rows >= 0) & (local_rows < rows_dev)
    chosen = fetched[jnp.clip(local_rows, 0, rows_dev - 1)]
    return jnp.where(inside[:, None], chosen, jnp.zeros_like(chosen))


def backward_solve(inverse_rows, solved, pulled, row_mask, active):
    scaled = ((solved.astype(jnp.float32) - pulled) * row_mask).astype(jnp.bfloat16)
    rhs_width = scaled.shape[1]
    row_count = inverse_rows.shape[0] * lax.axis_size("col")

    def rows_compute():
        return lax.dot_general(
            inverse_rows, scaled, (((0,), (0,)), ((), ())), preferred_element_type=jnp.float32
        )

    summed = lax.psum_scatter(
        lax.cond(active, rows_compute, lambda: jnp.zeros((row_count, rhs_width), jnp.float32)),
        "col",
        scatter_dimension=0,
        tiled=True,
    )
    return (summed * row_mask).astype(jnp.bfloat16)


def pull_terms(update_cols, tiles, active):

    def pull_compute():
        return jnp.einsum("srt,stn->rn", update_cols, tiles, preferred_element_type=jnp.float32)

    def pull_nothing():
        return jnp.zeros((update_cols.shape[1], tiles.shape[2]), jnp.float32)

    return lax.cond(active, pull_compute, pull_nothing)


def deliver(outgoing, height, leaf_id, leaf_count):
    owner = leaf_id // 2**height * 2**height + 2 ** (height - 1)
    onehot = (jnp.arange(leaf_count, dtype=jnp.int32) == owner).astype(jnp.float32)
    slot_table = onehot[:, None, None] * outgoing[None]
    return lax.psum_scatter(slot_table, "leaf", scatter_dimension=0, tiled=True)[0]


def fetch(answer_up, height, leaf_id):
    owner = leaf_id // 2**height * 2**height + 2 ** (height - 1)
    gathered = lax.all_gather(answer_up[None], "leaf", axis=0, tiled=True)
    return lax.dynamic_index_in_dim(gathered, owner, 0, keepdims=False)


def shards(
    right_sides, leaf_inverse, upper_inverse, leaf_update, upper_update, live_rows, tile_map
):
    leaf_count = lax.axis_size("leaf")
    depth = leaf_count.bit_length() - 1
    rows_dev = leaf_inverse.shape[1]
    rhs_width = right_sides.shape[3]
    tile_len = tile_map.shape[3]
    leaf_id = lax.axis_index("leaf")
    col_id = lax.axis_index("col")
    first_row = col_id * rows_dev
    row_ids = first_row + jnp.arange(rows_dev, dtype=jnp.int32)
    leaf_mask = (row_ids < live_rows[0, 0]).astype(jnp.float32)[:, None]
    upper_mask = (row_ids < live_rows[0, 1]).astype(jnp.float32)[:, None]
    node_level = jnp.zeros((), jnp.int32)
    for height in range(1, depth + 1):
        node_level = node_level + ((leaf_id % 2 ** (height - 1) == 0) & (leaf_id > 0)).astype(
            jnp.int32
        )
    always = jnp.array(True)
    solved_leaf = forward_solve(
        leaf_inverse[0], right_sides[0, 0].astype(jnp.float32), leaf_mask, always
    )
    summed = tile_terms(leaf_update[0, :depth], solved_leaf, always)
    pieces = spread(summed, tile_map[0, 0, :depth], first_row, rows_dev)
    outgoing = [None] + [pieces[height - 1] for height in range(1, depth + 1)]
    residual_up = right_sides[0, 1].astype(jnp.float32)
    solved_up = jnp.zeros((rows_dev, rhs_width), jnp.bfloat16)
    for height in range(1, depth + 1):
        residual_up = residual_up - deliver(outgoing[height], height, leaf_id, leaf_count)
        active = node_level == height
        solved = forward_solve(upper_inverse[0], residual_up, upper_mask, active)
        solved_up = jnp.where(active, solved, solved_up)
        slot_count = depth - height
        if slot_count > 0:
            summed = tile_terms(upper_update[0, :slot_count], solved, active)
            pieces = spread(summed, tile_map[0, 1, :slot_count], first_row, rows_dev)
            for slot_idx in range(slot_count):
                outgoing[height + 1 + slot_idx] = outgoing[height + 1 + slot_idx] + pieces[slot_idx]
    answer_up = jnp.zeros((rows_dev, rhs_width), jnp.bfloat16)
    tiles_leaf = [None] * depth
    tiles_upper = jnp.zeros((depth, tile_len, rhs_width), jnp.bfloat16)
    for height in range(depth, 0, -1):
        active = node_level == height
        slot_count = depth - height
        if slot_count > 0:
            pulled = pull_terms(upper_update[0, :slot_count], tiles_upper[:slot_count], active)
        else:
            pulled = jnp.zeros((rows_dev, rhs_width), jnp.float32)
        answer = backward_solve(upper_inverse[0], solved_up, pulled, upper_mask, active)
        answer_up = jnp.where(active, answer, answer_up)
        fetched = fetch(answer_up, height, leaf_id)
        slot_now = jnp.clip(height - node_level - 1, 0, depth - 1)
        valid = (node_level > 0) & (node_level < height)
        upper_map = lax.dynamic_index_in_dim(tile_map[0, 1], slot_now, 0, keepdims=False)
        leaf_part = pick_rows(fetched, tile_map[0, 0, height - 1], first_row, rows_dev)
        upper_part = pick_rows(fetched, upper_map, first_row, rows_dev)
        upper_part = jnp.where(valid, upper_part, jnp.zeros_like(upper_part))
        both = (
            lax.psum(jnp.stack([leaf_part, upper_part]), "col")
            .astype(jnp.float32)
            .astype(jnp.bfloat16)
        )
        tiles_leaf[height - 1] = both[0]
        updated = lax.dynamic_update_index_in_dim(tiles_upper, both[1], slot_now, 0)
        tiles_upper = jnp.where(valid, updated, tiles_upper)
    pulled = pull_terms(leaf_update[0, :depth], jnp.stack(tiles_leaf), always)
    answer_leaf = backward_solve(leaf_inverse[0], solved_leaf, pulled, leaf_mask, always)
    return jnp.stack([answer_leaf, answer_up])[None]


def solution(mesh):
    placed = (
        P("leaf", None, "col", None),
        P("leaf", "col", None),
        P("leaf", "col", None),
        P("leaf", None, "col", None),
        P("leaf", None, "col", None),
        P("leaf", None),
        P("leaf", None, None, None),
    )
    return jax.shard_map(
        shards, mesh=mesh, in_specs=placed, out_specs=P("leaf", None, "col", None), check_vma=False
    )
```

profile of v0, /device:TPU:4, one launch (start us, length us, event | category | flops | bytes accessed | tf_op | source)
XLA Modules:
  0.0 1755.9 jit_solution(690837087671866343)
XLA Ops:
  6.5 1.4 fusion.78
  9.4 21.2 %all_gather.27 = bf16[1792,128]{1,0:T(8,128)(2,1)S(1)} all-gather(bf16[112,128]{1,0:T(8,128)(2,1)S(1)} %fusion.53), channel_id=1, replica_groups=mesh['leaf'=16,'col'=16] {'col'}, dimensions={0}, use_global_device_ids=true | all-gather | bytes 487424 | tf_op jit(solution)/shard_map/all_gather | solution.py:10
  34.5 108.2 %all-reduce.13.cloned.1.call-done = f32[4,512,128]{1,2,0:T(8,128)} async-done(((f32[4,512,128]{1,2,0:T(8,128)}), f32[4,512,128]{1,2,0:T(8,128)}) %all-reduce.13.cloned.1.call-update) | async-done | bytes 1048592 | tf_op jit(solution)/shard_map/psum | solution.py:28
  142.7 1.5 copy.73
  144.3 11.5 scatter_custom_fusion.1
  158.6 77.5 %reduce-scatter.38.cloned.1.call-done = f32[1,112,128]{2,1,0:T(8,128)} async-done(((f32[16,112,128]{2,1,0:T(8,128)}), f32[1,112,128]{2,1,0:T(8,128)}) %reduce-scatter.38.cloned.1.call-update) | async-done | bytes 57360
  237.0 18.7 %all_gather.28 = bf16[1792,128]{1,0:T(8,128)(2,1)S(1)} all-gather(bf16[112,128]{1,0:T(8,128)(2,1)S(1)} %multiply_convert_fusion.11), channel_id=1, replica_groups=mesh['leaf'=16,'col'=16] {'col'}, dimensions={0}, use_global_device_ids=true | all-gather | bytes 487424 | tf_op jit(solution)/shard_map/all_gather | solution.py:10
  257.0 109.0 %all-reduce.15.cloned.1.call-done = f32[3,512,128]{2,1,0:T(8,128)} async-done(((f32[3,512,128]{2,1,0:T(8,128)}), f32[3,512,128]{2,1,0:T(8,128)}) %all-reduce.15.cloned.1.call-update) | async-done | bytes 786448 | tf_op jit(solution)/shard_map/psum | solution.py:28
  366.0 9.1 scatter_custom_fusion.2
  377.1 78.3 %reduce-scatter.40.cloned.1.call-done = f32[1,112,128]{2,1,0:T(8,128)} async-done(((f32[16,112,128]{2,1,0:T(8,128)}), f32[1,112,128]{2,1,0:T(8,128)}) %reduce-scatter.40.cloned.1.call-update) | async-done | bytes 57360
  456.3 18.7 %all_gather.29 = bf16[1792,128]{1,0:T(8,128)(2,1)S(1)} all-gather(bf16[112,128]{1,0:T(8,128)(2,1)S(1)} %get-tuple-element.234), channel_id=1, replica_groups=mesh['leaf'=16,'col'=16] {'col'}, dimensions={0}, use_global_device_ids=true | all-gather | bytes 487424 | tf_op jit(solution)/shard_map/all_gather | solution.py:10
  476.6 107.9 %all-reduce.17.cloned.1.call-done = f32[2,512,128]{2,1,0:T(8,128)} async-done(((f32[2,512,128]{2,1,0:T(8,128)}), f32[2,512,128]{2,1,0:T(8,128)}) %all-reduce.17.cloned.1.call-update) | async-done | bytes 524304 | tf_op jit(solution)/shard_map/psum | solution.py:28
  584.4 6.4 scatter_custom_fusion.3
  592.1 79.1 %reduce-scatter.42.cloned.1.call-done = f32[1,112,128]{2,1,0:T(8,128)} async-done(((f32[16,112,128]{2,1,0:T(8,128)}), f32[1,112,128]{2,1,0:T(8,128)}) %reduce-scatter.42.cloned.1.call-update) | async-done | bytes 57360
  672.2 18.7 %all_gather.30 = bf16[1792,128]{1,0:T(8,128)(2,1)S(1)} all-gather(bf16[112,128]{1,0:T(8,128)(2,1)S(1)} %multiply_convert_fusion.7), channel_id=1, replica_groups=mesh['leaf'=16,'col'=16] {'col'}, dimensions={0}, use_global_device_ids=true | all-gather | bytes 487424 | tf_op jit(solution)/shard_map/all_gather | solution.py:10
  691.8 106.9 %all-reduce.19.cloned.1.call-done = f32[1,512,128]{2,1,0:T(8,128)} async-done(((f32[1,512,128]{2,1,0:T(8,128)}), f32[1,512,128]{2,1,0:T(8,128)}) %all-reduce.19.cloned.1.call-update) | async-done | bytes 262160 | tf_op jit(solution)/shard_map/psum | solution.py:28
  798.7 3.9 scatter_custom_fusion
  803.8 79.3 %reduce-scatter.44.cloned.1.call-done = f32[1,112,128]{2,1,0:T(8,128)} async-done(((f32[16,112,128]{2,1,0:T(8,128)}), f32[1,112,128]{2,1,0:T(8,128)}) %reduce-scatter.44.cloned.1.call-update) | async-done | bytes 57360
  884.0 18.7 %all_gather.31 = bf16[1792,128]{1,0:T(8,128)(2,1)S(1)} all-gather(bf16[112,128]{1,0:T(8,128)(2,1)S(1)} %fusion.55), channel_id=1, replica_groups=mesh['leaf'=16,'col'=16] {'col'}, dimensions={0}, use_global_device_ids=true | all-gather | bytes 487424 | tf_op jit(solution)/shard_map/all_gather | solution.py:10
  906.3 52.8 %reduce-scatter.28.cloned.1.call-done = f32[112,128]{1,0:T(8,128)} async-done(((f32[1792,128]{1,0:T(8,128)}), f32[112,128]{1,0:T(8,128)}) %reduce-scatter.28.cloned.1.call-update) | async-done | bytes 57360 | tf_op jit(solution)/shard_map/reduce_scatter | solution.py:63
  960.0 23.5 %all-gather = bf16[1792,128]{1,0:T(8,128)(2,1)S(1)} all-gather(bf16[112,128]{1,0:T(8,128)(2,1)S(1)} %fusion.60), channel_id=2, replica_groups=mesh['leaf'=16,'col'=16] {'leaf'}, dimensions={0}, use_global_device_ids=true | all-gather | bytes 487424 | tf_op jit(solution)/shard_map/all_gather | solution.py:92
  987.3 107.1 %all-reduce.21.cloned.1.call-done = bf16[2,512,128]{2,1,0:T(8,128)(2,1)} async-done(((bf16[2,512,128]{2,1,0:T(8,128)(2,1)}), bf16[2,512,128]{2,1,0:T(8,128)(2,1)}) %all-reduce.21.cloned.1.call-update) | async-done | bytes 262160 | tf_op jit(solution)/shard_map/psum | solution.py:155
  1096.6 58.6 %reduce-scatter.30.cloned.1.call-done = f32[112,128]{1,0:T(8,128)} async-done(((f32[1792,128]{1,0:T(8,128)}), f32[112,128]{1,0:T(8,128)}) %reduce-scatter.30.cloned.1.call-update) | async-done | bytes 57360 | tf_op jit(solution)/shard_map/reduce_scatter | solution.py:63
  1156.2 23.6 %all-gather.1 = bf16[1792,128]{1,0:T(8,128)(2,1)S(1)} all-gather(bf16[112,128]{1,0:T(8,128)(2,1)S(1)} %fusion.61), channel_id=3, replica_groups=mesh['leaf'=16,'col'=16] {'leaf'}, dimensions={0}, use_global_device_ids=true | all-gather | bytes 487424 | tf_op jit(solution)/shard_map/all_gather | solution.py:92
  1183.5 107.0 %all-reduce.23.cloned.1.call-done = bf16[2,512,128]{2,1,0:T(8,128)(2,1)} async-done(((bf16[2,512,128]{2,1,0:T(8,128)(2,1)}), bf16[2,512,128]{2,1,0:T(8,128)(2,1)}) %all-reduce.23.cloned.1.call-update) | async-done | bytes 262160 | tf_op jit(solution)/shard_map/psum | solution.py:155
  1293.9 58.4 %reduce-scatter.32.cloned.1.call-done = f32[112,128]{1,0:T(8,128)} async-done(((f32[1792,128]{1,0:T(8,128)}), f32[112,128]{1,0:T(8,128)}) %reduce-scatter.32.cloned.1.call-update) | async-done | bytes 57360 | tf_op jit(solution)/shard_map/reduce_scatter | solution.py:63
  1353.1 23.6 %all-gather.2 = bf16[1792,128]{1,0:T(8,128)(2,1)S(1)} all-gather(bf16[112,128]{1,0:T(8,128)(2,1)S(1)} %fusion.62), channel_id=4, replica_groups=mesh['leaf'=16,'col'=16] {'leaf'}, dimensions={0}, use_global_device_ids=true | all-gather | bytes 487424 | tf_op jit(solution)/shard_map/all_gather | solution.py:92
  1381.7 107.2 %all-reduce.25.cloned.1.call-done = bf16[2,512,128]{2,1,0:T(8,128)(2,1)} async-done(((bf16[2,512,128]{2,1,0:T(8,128)(2,1)}), bf16[2,512,128]{2,1,0:T(8,128)(2,1)}) %all-reduce.25.cloned.1.call-update) | async-done | bytes 262160 | tf_op jit(solution)/shard_map/psum | solution.py:155
  1491.0 58.9 %reduce-scatter.34.cloned.1.call-done = f32[112,128]{1,0:T(8,128)} async-done(((f32[1792,128]{1,0:T(8,128)}), f32[112,128]{1,0:T(8,128)}) %reduce-scatter.34.cloned.1.call-update) | async-done | bytes 57360 | tf_op jit(solution)/shard_map/reduce_scatter | solution.py:63
  1550.7 23.6 %all-gather.3 = bf16[1792,128]{1,0:T(8,128)(2,1)S(1)} all-gather(bf16[112,128]{1,0:T(8,128)(2,1)S(1)} %fusion.63), channel_id=5, replica_groups=mesh['leaf'=16,'col'=16] {'leaf'}, dimensions={0}, use_global_device_ids=true | all-gather | bytes 487424 | tf_op jit(solution)/shard_map/all_gather | solution.py:92
  1580.2 106.1 %all-reduce.27.cloned.1.call-done = bf16[2,512,128]{2,1,0:T(8,128)(2,1)} async-done(((bf16[2,512,128]{2,1,0:T(8,128)(2,1)}), bf16[2,512,128]{2,1,0:T(8,128)(2,1)}) %all-reduce.27.cloned.1.call-update) | async-done | bytes 262160 | tf_op jit(solution)/shard_map/psum | solution.py:155
  1689.1 58.7 %reduce-scatter.36.cloned.1.call-done = f32[112,128]{1,0:T(8,128)} async-done(((f32[1792,128]{1,0:T(8,128)}), f32[112,128]{1,0:T(8,128)}) %reduce-scatter.36.cloned.1.call-update) | async-done | bytes 57360 | tf_op jit(solution)/shard_map/reduce_scatter | solution.py:63
  (233 shorter events, 57.5 us)
Async XLA Ops:
  6.5 24.4 %copy-start = (bf16[1,4,112,512]{3,2,1,0:T(8,128)(2,1)S(1)}, bf16[1,4,112,512]{3,2,1,0:T(8,128)(2,1)}, u32[]{:S(2)}) copy-start(bf16[1,4,112,512]{3,2,1,0:T(8,128)(2,1)} %param.38) | copy-start | bytes 1376260
  6.5 24.1 %copy-start.8 = (bf16[1,112,1792]{2,1,0:T(8,128)(2,1)S(1)}, bf16[1,112,1792]{2,1,0:T(8,128)(2,1)}, u32[]{:S(2)}) copy-start(bf16[1,112,1792]{2,1,0:T(8,128)(2,1)} %param.36) | copy-start | bytes 1204228
  6.5 136.2 %all-reduce.13.cloned.1.call-start = ((), (), s32[]{:S(2)}) async-start(), calls=%async_computation.9 | async-start | bytes 2097152 | tf_op jit(solution)/shard_map/psum | solution.py:28
  31.0 1.3 copy-start.16
  32.3 203.8 %reduce-scatter.38.cloned.1.call-start = ((), (), s32[]{:S(2)}) async-start(), calls=%async_computation.22 | async-start | bytes 974848
  156.9 1.6 copy-start.10
  156.9 209.0 %all-reduce.15.cloned.1.call-start = ((), (), s32[]{:S(2)}) async-start(), calls=%async_computation.10 | async-start | bytes 1572864 | tf_op jit(solution)/shard_map/psum | solution.py:28
  158.5 77.6 %copy-start.24 = (bf16[1,2,112,128]{3,2,1,0:T(8,128)(2,1)S(1)}, bf16[1,2,112,128]{3,2,1,0:T(8,128)(2,1)}, u32[]{:S(2)}) copy-start(bf16[1,2,112,128]{3,2,1,0:T(8,128)(2,1)} %param.35) | copy-start | bytes 172036
  158.6 97.1 %copy-start.1 = (bf16[1,112,1792]{2,1,0:T(8,128)(2,1)S(1)}, bf16[1,112,1792]{2,1,0:T(8,128)(2,1)}, u32[]{:S(2)}) copy-start(bf16[1,112,1792]{2,1,0:T(8,128)(2,1)} %param.37) | copy-start | bytes 1204228
  256.8 198.6 %reduce-scatter.40.cloned.1.call-start = ((), (), s32[]{:S(2)}) async-start(), calls=%async_computation.23 | async-start | bytes 974848
  376.2 208.2 %all-reduce.17.cloned.1.call-start = ((), (), s32[]{:S(2)}) async-start(), calls=%async_computation.11 | async-start | bytes 1048576 | tf_op jit(solution)/shard_map/psum | solution.py:28
  377.1 78.4 %copy-start.20 = (f32[1,112,128]{2,1,0:T(8,128)S(1)}, f32[1,112,128]{2,1,0:T(8,128)}, u32[]{:S(2)}) copy-start(f32[1,112,128]{2,1,0:T(8,128)} %reduce-scatter.38.cloned.1.call-done) | copy-start | bytes 172036
  476.5 194.8 %reduce-scatter.42.cloned.1.call-start = ((), (), s32[]{:S(2)}) async-start(), calls=%async_computation.24 | async-start | bytes 974848
  592.0 206.7 %all-reduce.19.cloned.1.call-start = ((), (), s32[]{:S(2)}) async-start(), calls=%async_computation.12 | async-start | bytes 524288 | tf_op jit(solution)/shard_map/psum | solution.py:28
  691.7 191.4 %reduce-scatter.44.cloned.1.call-start = ((), (), s32[]{:S(2)}) async-start(), calls=%async_computation.25 | async-start | bytes 974848
  803.7 79.4 %copy-start.22 = (f32[1,112,128]{2,1,0:T(8,128)S(1)}, f32[1,112,128]{2,1,0:T(8,128)}, u32[]{:S(2)}) copy-start(f32[1,112,128]{2,1,0:T(8,128)} %reduce-scatter.42.cloned.1.call-done) | copy-start | bytes 172036
  803.7 155.4 %reduce-scatter.28.cloned.1.call-start = ((), (), s32[]{:S(2)}) async-start(), calls=%async_computation.17 | async-start | bytes 974848 | tf_op jit(solution)/shard_map/reduce_scatter | solution.py:63
  902.8 192.6 %copy-start.11 = (bf16[112,128]{1,0:T(8,128)(2,1)}, bf16[112,128]{1,0:T(8,128)(2,1)S(1)}, u32[]{:S(2)}) copy-start(bf16[112,128]{1,0:T(8,128)(2,1)S(1)} %get-tuple-element.233) | copy-start | bytes 86020
  903.8 190.5 %all-reduce.21.cloned.1.call-start = ((), (), s32[]{:S(2)}) async-start(), calls=%async_computation.13 | async-start | bytes 524288 | tf_op jit(solution)/shard_map/psum | solution.py:155
  987.2 168.0 %reduce-scatter.30.cloned.1.call-start = ((), (), s32[]{:S(2)}) async-start(), calls=%async_computation.18 | async-start | bytes 974848 | tf_op jit(solution)/shard_map/reduce_scatter | solution.py:63
  1095.6 59.7 %copy-start.21 = (f32[112,128]{1,0:T(8,128)S(1)}, f32[112,128]{1,0:T(8,128)}, u32[]{:S(2)}) copy-start(f32[112,128]{1,0:T(8,128)} %reduce-scatter.28.cloned.1.call-done) | copy-start | bytes 172036
  1096.5 194.1 %all-reduce.23.cloned.1.call-start = ((), (), s32[]{:S(2)}) async-start(), calls=%async_computation.14 | async-start | bytes 524288 | tf_op jit(solution)/shard_map/psum | solution.py:155
  1156.1 23.6 %copy-start.18 = (bf16[112,128]{1,0:T(8,128)(2,1)}, bf16[112,128]{1,0:T(8,128)(2,1)S(1)}, u32[]{:S(2)}) copy-start(bf16[112,128]{1,0:T(8,128)(2,1)S(1)} %fusion.61) | copy-start | bytes 86020
  1183.5 168.7 %reduce-scatter.32.cloned.1.call-start = ((), (), s32[]{:S(2)}) async-start(), calls=%async_computation.19 | async-start | bytes 974848 | tf_op jit(solution)/shard_map/reduce_scatter | solution.py:63
  1292.8 1.0 copy-start.26
  1292.8 1.1 copy-start.25
  1293.7 58.5 %copy-start.19 = (bf16[112,128]{1,0:T(8,128)(2,1)S(1)}, bf16[112,128]{1,0:T(8,128)(2,1)}, u32[]{:S(2)}) copy-start(bf16[112,128]{1,0:T(8,128)(2,1)} %copy-done.18) | copy-start | bytes 86020
  1293.8 195.2 %all-reduce.25.cloned.1.call-start = ((), (), s32[]{:S(2)}) async-start(), calls=%async_computation.15 | async-start | bytes 524288 | tf_op jit(solution)/shard_map/psum | solution.py:155
  1381.7 168.1 %reduce-scatter.34.cloned.1.call-start = ((), (), s32[]{:S(2)}) async-start(), calls=%async_computation.20 | async-start | bytes 974848 | tf_op jit(solution)/shard_map/reduce_scatter | solution.py:63
  1490.9 195.5 %all-reduce.27.cloned.1.call-start = ((), (), s32[]{:S(2)}) async-start(), calls=%async_computation.16 | async-start | bytes 524288 | tf_op jit(solution)/shard_map/psum | solution.py:155
  1579.3 168.5 %reduce-scatter.36.cloned.1.call-start = ((), (), s32[]{:S(2)}) async-start(), calls=%async_computation.21 | async-start | bytes 974848 | tf_op jit(solution)/shard_map/reduce_scatter | solution.py:63
  1580.2 106.1 %copy-start.17 = (bf16[128,112]{0,1:T(8,128)(2,1)S(1)}, bf16[128,112]{0,1:T(8,128)(2,1)}, u32[]{:S(2)}) copy-start(bf16[128,112]{0,1:T(8,128)(2,1)} %copy-done.16) | copy-start | bytes 86020
  (21 other events, 16.3 us)
Sparse Core Ops, SparseCore 0:
  32.4 110.2 all-reduce.12
  157.1 78.9 reduce-scatter.37
  256.9 108.9 all-reduce.14
  376.3 79.0 reduce-scatter.39
  476.6 107.7 all-reduce.16
  592.1 79.0 reduce-scatter.41
  691.8 106.8 all-reduce.18
  803.8 79.1 reduce-scatter.43
  903.9 55.1 reduce-scatter.27
  987.3 106.9 all-reduce.20
  1096.9 58.3 reduce-scatter.29
  1183.6 106.9 all-reduce.22
  1293.9 58.3 reduce-scatter.31
  1381.8 107.1 all-reduce.24
  1491.3 58.4 reduce-scatter.33
  1579.4 106.9 all-reduce.26
  1689.2 58.5 reduce-scatter.35
where the time goes:
time: 1760 us
  waiting for transfers between devices  1460 us (83%)
  blocking collectives  190 us (11%)
  other arithmetic  54.8 us (3%)
  local copies, waits for them, and re-layouts  31.1 us (2%)
    psum x4, waiting for transfers between devices, tile_terms(): return lax.psum(local_terms, 'col')  432 us
    psum x4, waiting for transfers between devices, shards(): lax.psum(jnp.stack([leaf_part, upper_part]), 'col').astype(jnp.float32)  427 us
    unnamed x21, waiting for transfers between devices  315 us
    reduce_scatter x5, waiting for transfers between devices, backward_solve(): lax.psum_scatter(lax.cond(active, rows_compute, lambda: jnp.zeros((row_co...  287 us
    all_gather x5, blocking collectives, forward_solve(): shard_rows = lax.all_gather(shares, 'col', axis=0, tiled=True)  96 us
    all_gather x4, blocking collectives, fetch(): gathered = lax.all_gather(answer_up[None], 'leaf', axis=0, tiled=True)  94.3 us
  transfers between devices with their start and end apart: 17, of which 17 were waited for; matrix products, arithmetic and copies ran while one was open for 0% of the time, Pallas kernels for 0%

commit v1 on v0

--- a/solution.py
+++ b/solution.py
@@ -89,7 +89,16 @@
 
 def fetch(answer_up, height, leaf_id):
     owner = leaf_id // 2**height * 2**height + 2 ** (height - 1)
-    gathered = lax.all_gather(answer_up[None], "leaf", axis=0, tiled=True)
+    body = answer_up[None]
+    gathered = jnp.concatenate(
+        lax.all_to_all(
+            jnp.stack([body] * lax.axis_size("leaf"), axis=0),
+            axis_name="leaf",
+            split_axis=0,
+            concat_axis=0,
+        ),
+        0,
+    )
     return lax.dynamic_index_in_dim(gathered, owner, 0, keepdims=False)
 
 

time: 1760 us -> 1730 us (0.983)
  blocking collectives: 190 us -> 96 us
  waiting for transfers between devices: 1460 us -> 1490 us
  starting transfers between devices: 0.67 us -> 29.7 us
    all_gather x4 -> x0, blocking collectives: 94.3 us -> none  [fetch(): gathered = lax.all_gather(answer_up[None], 'leaf', axis=0, tiled=True)]
    all_to_all x0 -> x4, starting transfers between devices: none -> 29.1 us  [fetch(): lax.all_to_all(jnp.stack([body] * lax.axis_size('leaf'), axis=0), axis_na...]
    all_to_all x0 -> x4, waiting for transfers between devices: none -> 25.8 us  [fetch(): lax.all_to_all(jnp.stack([body] * lax.axis_size('leaf'), axis=0), axis_na...]
  transfers between devices with their start and end apart: 17 -> 21, of which waited for: 17 -> 21; matrix products, arithmetic and copies ran while one was open for 0% -> 0% of each run, Pallas kernels for 0% -> 0%
where the time goes in v1:
time: 1730 us
  waiting for transfers between devices  1490 us (86%)
  blocking collectives  96 us (6%)
  other arithmetic  54.8 us (3%)
  local copies, waits for them, and re-layouts  35.8 us (2%)
  starting transfers between devices  29.7 us (2%)
    psum x4, waiting for transfers between devices, tile_terms(): return lax.psum(local_terms, 'col')  432 us
    psum x4, waiting for transfers between devices, shards(): lax.psum(jnp.stack([leaf_part, upper_part]), 'col').astype(jnp.float32)  431 us
    unnamed x21, waiting for transfers between devices  315 us
    reduce_scatter x5, waiting for transfers between devices, backward_solve(): lax.psum_scatter(lax.cond(active, rows_compute, lambda: jnp.zeros((row_co...  289 us
    all_gather x5, blocking collectives, forward_solve(): shard_rows = lax.all_gather(shares, 'col', axis=0, tiled=True)  96 us
  transfers between devices with their start and end apart: 21, of which 21 were waited for; matrix products, arithmetic and copies ran while one was open for 0% of the time, Pallas kernels for 0%

profile of v1, /device:TPU:4, one launch (start us, length us, event | category | flops | bytes accessed | tf_op | source)
XLA Modules:
  0.0 1726.0 jit_solution(9505569677209155708)
XLA Ops:
  9.4 21.2 %all_gather.15 = bf16[1792,128]{1,0:T(8,128)(2,1)S(1)} all-gather(bf16[112,128]{1,0:T(8,128)(2,1)S(1)} %fusion.53), channel_id=1, replica_groups=mesh['leaf'=16,'col'=16] {'col'}, dimensions={0}, use_global_device_ids=true | all-gather | bytes 487424 | tf_op jit(solution)/shard_map/all_gather | solution.py:10
  34.5 108.2 %all-reduce.13.cloned.1.call-done = f32[4,512,128]{1,2,0:T(8,128)} async-done(((f32[4,512,128]{1,2,0:T(8,128)}), f32[4,512,128]{1,2,0:T(8,128)}) %all-reduce.13.cloned.1.call-update) | async-done | bytes 1048592 | tf_op jit(solution)/shard_map/psum | solution.py:28
  144.3 11.5 scatter_custom_fusion.1
  158.5 77.6 %reduce-scatter.38.cloned.1.call-done = f32[1,112,128]{2,1,0:T(8,128)} async-done(((f32[16,112,128]{2,1,0:T(8,128)}), f32[1,112,128]{2,1,0:T(8,128)}) %reduce-scatter.38.cloned.1.call-update) | async-done | bytes 57360
  237.0 18.7 %all_gather.16 = bf16[1792,128]{1,0:T(8,128)(2,1)S(1)} all-gather(bf16[112,128]{1,0:T(8,128)(2,1)S(1)} %multiply_convert_fusion.11), channel_id=1, replica_groups=mesh['leaf'=16,'col'=16] {'col'}, dimensions={0}, use_global_device_ids=true | all-gather | bytes 487424 | tf_op jit(solution)/shard_map/all_gather | solution.py:10
  257.0 109.0 %all-reduce.15.cloned.1.call-done = f32[3,512,128]{2,1,0:T(8,128)} async-done(((f32[3,512,128]{2,1,0:T(8,128)}), f32[3,512,128]{2,1,0:T(8,128)}) %all-reduce.15.cloned.1.call-update) | async-done | bytes 786448 | tf_op jit(solution)/shard_map/psum | solution.py:28
  366.0 9.1 scatter_custom_fusion.2
  377.1 78.3 %reduce-scatter.40.cloned.1.call-done = f32[1,112,128]{2,1,0:T(8,128)} async-done(((f32[16,112,128]{2,1,0:T(8,128)}), f32[1,112,128]{2,1,0:T(8,128)}) %reduce-scatter.40.cloned.1.call-update) | async-done | bytes 57360
  456.3 18.7 %all_gather.17 = bf16[1792,128]{1,0:T(8,128)(2,1)S(1)} all-gather(bf16[112,128]{1,0:T(8,128)(2,1)S(1)} %get-tuple-element.234), channel_id=1, replica_groups=mesh['leaf'=16,'col'=16] {'col'}, dimensions={0}, use_global_device_ids=true | all-gather | bytes 487424 | tf_op jit(solution)/shard_map/all_gather | solution.py:10
  476.6 107.9 %all-reduce.17.cloned.1.call-done = f32[2,512,128]{2,1,0:T(8,128)} async-done(((f32[2,512,128]{2,1,0:T(8,128)}), f32[2,512,128]{2,1,0:T(8,128)}) %all-reduce.17.cloned.1.call-update) | async-done | bytes 524304 | tf_op jit(solution)/shard_map/psum | solution.py:28
  584.5 6.4 scatter_custom_fusion.3
  592.1 79.1 %reduce-scatter.42.cloned.1.call-done = f32[1,112,128]{2,1,0:T(8,128)} async-done(((f32[16,112,128]{2,1,0:T(8,128)}), f32[1,112,128]{2,1,0:T(8,128)}) %reduce-scatter.42.cloned.1.call-update) | async-done | bytes 57360
  672.2 18.7 %all_gather.18 = bf16[1792,128]{1,0:T(8,128)(2,1)S(1)} all-gather(bf16[112,128]{1,0:T(8,128)(2,1)S(1)} %multiply_convert_fusion.7), channel_id=1, replica_groups=mesh['leaf'=16,'col'=16] {'col'}, dimensions={0}, use_global_device_ids=true | all-gather | bytes 487424 | tf_op jit(solution)/shard_map/all_gather | solution.py:10
  691.9 106.9 %all-reduce.19.cloned.1.call-done = f32[1,512,128]{2,1,0:T(8,128)} async-done(((f32[1,512,128]{2,1,0:T(8,128)}), f32[1,512,128]{2,1,0:T(8,128)}) %all-reduce.19.cloned.1.call-update) | async-done | bytes 262160 | tf_op jit(solution)/shard_map/psum | solution.py:28
  803.8 79.3 %reduce-scatter.44.cloned.1.call-done = f32[1,112,128]{2,1,0:T(8,128)} async-done(((f32[16,112,128]{2,1,0:T(8,128)}), f32[1,112,128]{2,1,0:T(8,128)}) %reduce-scatter.44.cloned.1.call-update) | async-done | bytes 57360
  884.0 18.7 %all_gather.19 = bf16[1792,128]{1,0:T(8,128)(2,1)S(1)} all-gather(bf16[112,128]{1,0:T(8,128)(2,1)S(1)} %fusion.55), channel_id=1, replica_groups=mesh['leaf'=16,'col'=16] {'col'}, dimensions={0}, use_global_device_ids=true | all-gather | bytes 487424 | tf_op jit(solution)/shard_map/all_gather | solution.py:10
  905.2 54.0 %reduce-scatter.28.cloned.1.call-done = f32[112,128]{1,0:T(8,128)} async-done(((f32[1792,128]{1,0:T(8,128)}), f32[112,128]{1,0:T(8,128)}) %reduce-scatter.28.cloned.1.call-update) | async-done | bytes 57360 | tf_op jit(solution)/shard_map/reduce_scatter | solution.py:63
  960.9 7.3 all-to-all-start
  969.4 5.9 all-to-all-done
  979.1 107.8 %all-reduce.21.cloned.1.call-done = bf16[2,512,128]{2,1,0:T(8,128)(2,1)} async-done(((bf16[2,512,128]{2,1,0:T(8,128)(2,1)}), bf16[2,512,128]{2,1,0:T(8,128)(2,1)}) %all-reduce.21.cloned.1.call-update) | async-done | bytes 262160 | tf_op jit(solution)/shard_map/psum | solution.py:164
  1089.1 58.7 %reduce-scatter.30.cloned.1.call-done = f32[112,128]{1,0:T(8,128)} async-done(((f32[1792,128]{1,0:T(8,128)}), f32[112,128]{1,0:T(8,128)}) %reduce-scatter.30.cloned.1.call-update) | async-done | bytes 57360 | tf_op jit(solution)/shard_map/reduce_scatter | solution.py:63
  1149.5 7.3 all-to-all-start.1
  1156.9 7.1 all-to-all-done.1
  1167.8 107.8 %all-reduce.23.cloned.1.call-done = bf16[2,512,128]{2,1,0:T(8,128)(2,1)} async-done(((bf16[2,512,128]{2,1,0:T(8,128)(2,1)}), bf16[2,512,128]{2,1,0:T(8,128)(2,1)}) %all-reduce.23.cloned.1.call-update) | async-done | bytes 262160 | tf_op jit(solution)/shard_map/psum | solution.py:164
  1278.8 58.5 %reduce-scatter.32.cloned.1.call-done = f32[112,128]{1,0:T(8,128)} async-done(((f32[1792,128]{1,0:T(8,128)}), f32[112,128]{1,0:T(8,128)}) %reduce-scatter.32.cloned.1.call-update) | async-done | bytes 57360 | tf_op jit(solution)/shard_map/reduce_scatter | solution.py:63
  1339.0 7.3 all-to-all-start.2
  1358.5 108.0 %all-reduce.25.cloned.1.call-done = bf16[2,512,128]{2,1,0:T(8,128)(2,1)} async-done(((bf16[2,512,128]{2,1,0:T(8,128)(2,1)}), bf16[2,512,128]{2,1,0:T(8,128)(2,1)}) %all-reduce.25.cloned.1.call-update) | async-done | bytes 262160 | tf_op jit(solution)/shard_map/psum | solution.py:164
  1468.4 58.9 %reduce-scatter.34.cloned.1.call-done = f32[112,128]{1,0:T(8,128)} async-done(((f32[1792,128]{1,0:T(8,128)}), f32[112,128]{1,0:T(8,128)}) %reduce-scatter.34.cloned.1.call-update) | async-done | bytes 57360 | tf_op jit(solution)/shard_map/reduce_scatter | solution.py:63
  1529.1 7.3 all-to-all-start.3
  1536.4 7.1 all-to-all-done.3
  1549.4 107.1 %all-reduce.27.cloned.1.call-done = bf16[2,512,128]{2,1,0:T(8,128)(2,1)} async-done(((bf16[2,512,128]{2,1,0:T(8,128)(2,1)}), bf16[2,512,128]{2,1,0:T(8,128)(2,1)}) %all-reduce.27.cloned.1.call-update) | async-done | bytes 262160 | tf_op jit(solution)/shard_map/psum | solution.py:164
  1659.3 58.7 %reduce-scatter.36.cloned.1.call-done = f32[112,128]{1,0:T(8,128)} async-done(((f32[1792,128]{1,0:T(8,128)}), f32[112,128]{1,0:T(8,128)}) %reduce-scatter.36.cloned.1.call-update) | async-done | bytes 57360 | tf_op jit(solution)/shard_map/reduce_scatter | solution.py:63
  (241 shorter events, 74.9 us)
Async XLA Ops:
  6.5 24.4 %copy-start = (bf16[1,4,112,512]{3,2,1,0:T(8,128)(2,1)S(1)}, bf16[1,4,112,512]{3,2,1,0:T(8,128)(2,1)}, u32[]{:S(2)}) copy-start(bf16[1,4,112,512]{3,2,1,0:T(8,128)(2,1)} %param.38) | copy-start | bytes 1376260
  6.5 24.1 %copy-start.8 = (bf16[1,112,1792]{2,1,0:T(8,128)(2,1)S(1)}, bf16[1,112,1792]{2,1,0:T(8,128)(2,1)}, u32[]{:S(2)}) copy-start(bf16[1,112,1792]{2,1,0:T(8,128)(2,1)} %param.36) | copy-start | bytes 1204228
  6.5 136.2 %all-reduce.13.cloned.1.call-start = ((), (), s32[]{:S(2)}) async-start(), calls=%async_computation.13 | async-start | bytes 2097152 | tf_op jit(solution)/shard_map/psum | solution.py:28
  32.3 203.8 %reduce-scatter.38.cloned.1.call-start = ((), (), s32[]{:S(2)}) async-start(), calls=%async_computation.26 | async-start | bytes 974848
  156.9 1.6 copy-start.10
  156.9 209.1 %all-reduce.15.cloned.1.call-start = ((), (), s32[]{:S(2)}) async-start(), calls=%async_computation.14 | async-start | bytes 1572864 | tf_op jit(solution)/shard_map/psum | solution.py:28
  158.5 77.6 %copy-start.24 = (bf16[1,2,112,128]{3,2,1,0:T(8,128)(2,1)S(1)}, bf16[1,2,112,128]{3,2,1,0:T(8,128)(2,1)}, u32[]{:S(2)}) copy-start(bf16[1,2,112,128]{3,2,1,0:T(8,128)(2,1)} %param.35) | copy-start | bytes 172036
  158.5 97.2 %copy-start.1 = (bf16[1,112,1792]{2,1,0:T(8,128)(2,1)S(1)}, bf16[1,112,1792]{2,1,0:T(8,128)(2,1)}, u32[]{:S(2)}) copy-start(bf16[1,112,1792]{2,1,0:T(8,128)(2,1)} %param.37) | copy-start | bytes 1204228
  256.8 198.6 %reduce-scatter.40.cloned.1.call-start = ((), (), s32[]{:S(2)}) async-start(), calls=%async_computation.27 | async-start | bytes 974848
  376.2 208.2 %all-reduce.17.cloned.1.call-start = ((), (), s32[]{:S(2)}) async-start(), calls=%async_computation.15 | async-start | bytes 1048576 | tf_op jit(solution)/shard_map/psum | solution.py:28
  377.1 78.4 %copy-start.20 = (f32[1,112,128]{2,1,0:T(8,128)S(1)}, f32[1,112,128]{2,1,0:T(8,128)}, u32[]{:S(2)}) copy-start(f32[1,112,128]{2,1,0:T(8,128)} %reduce-scatter.38.cloned.1.call-done) | copy-start | bytes 172036
  476.5 194.8 %reduce-scatter.42.cloned.1.call-start = ((), (), s32[]{:S(2)}) async-start(), calls=%async_computation.28 | async-start | bytes 974848
  592.0 206.7 %all-reduce.19.cloned.1.call-start = ((), (), s32[]{:S(2)}) async-start(), calls=%async_computation.16 | async-start | bytes 524288 | tf_op jit(solution)/shard_map/psum | solution.py:28
  691.8 191.4 %reduce-scatter.44.cloned.1.call-start = ((), (), s32[]{:S(2)}) async-start(), calls=%async_computation.29 | async-start | bytes 974848
  803.7 79.4 %copy-start.22 = (f32[1,112,128]{2,1,0:T(8,128)S(1)}, f32[1,112,128]{2,1,0:T(8,128)}, u32[]{:S(2)}) copy-start(f32[1,112,128]{2,1,0:T(8,128)} %reduce-scatter.42.cloned.1.call-done) | copy-start | bytes 172036
  803.8 155.4 %reduce-scatter.28.cloned.1.call-start = ((), (), s32[]{:S(2)}) async-start(), calls=%async_computation.21 | async-start | bytes 974848 | tf_op jit(solution)/shard_map/reduce_scatter | solution.py:63
  902.8 185.1 %copy-start.11 = (bf16[112,128]{1,0:T(8,128)(2,1)}, bf16[112,128]{1,0:T(8,128)(2,1)S(1)}, u32[]{:S(2)}) copy-start(bf16[112,128]{1,0:T(8,128)(2,1)S(1)} %get-tuple-element.233) | copy-start | bytes 86020
  960.9 14.4 all-to-all-start
  968.2 118.7 %all-reduce.21.cloned.1.call-start = ((), (), s32[]{:S(2)}) async-start(), calls=%async_computation.17 | async-start | bytes 524288 | tf_op jit(solution)/shard_map/psum | solution.py:164
  979.0 168.8 %reduce-scatter.30.cloned.1.call-start = ((), (), s32[]{:S(2)}) async-start(), calls=%async_computation.22 | async-start | bytes 974848 | tf_op jit(solution)/shard_map/reduce_scatter | solution.py:63
  1088.1 59.7 %copy-start.21 = (f32[112,128]{1,0:T(8,128)S(1)}, f32[112,128]{1,0:T(8,128)}, u32[]{:S(2)}) copy-start(f32[112,128]{1,0:T(8,128)} %reduce-scatter.28.cloned.1.call-done) | copy-start | bytes 172036
  1149.5 14.4 all-to-all-start.1
  1156.8 118.8 %all-reduce.23.cloned.1.call-start = ((), (), s32[]{:S(2)}) async-start(), calls=%async_computation.18 | async-start | bytes 524288 | tf_op jit(solution)/shard_map/psum | solution.py:164
  1167.7 169.5 %reduce-scatter.32.cloned.1.call-start = ((), (), s32[]{:S(2)}) async-start(), calls=%async_computation.23 | async-start | bytes 974848 | tf_op jit(solution)/shard_map/reduce_scatter | solution.py:63
  1277.8 59.5 %copy-start.19 = (bf16[112,128]{1,0:T(8,128)(2,1)S(1)}, bf16[112,128]{1,0:T(8,128)(2,1)}, u32[]{:S(2)}) copy-start(bf16[112,128]{1,0:T(8,128)(2,1)} %copy-done.18) | copy-start | bytes 86020
  1339.0 14.4 all-to-all-start.2
  1346.3 120.3 %all-reduce.25.cloned.1.call-start = ((), (), s32[]{:S(2)}) async-start(), calls=%async_computation.19 | async-start | bytes 524288 | tf_op jit(solution)/shard_map/psum | solution.py:164
  1358.4 168.9 %reduce-scatter.34.cloned.1.call-start = ((), (), s32[]{:S(2)}) async-start(), calls=%async_computation.24 | async-start | bytes 974848 | tf_op jit(solution)/shard_map/reduce_scatter | solution.py:63
  1529.1 14.4 all-to-all-start.3
  1536.4 120.2 %all-reduce.27.cloned.1.call-start = ((), (), s32[]{:S(2)}) async-start(), calls=%async_computation.20 | async-start | bytes 524288 | tf_op jit(solution)/shard_map/psum | solution.py:164
  1548.5 169.5 %reduce-scatter.36.cloned.1.call-start = ((), (), s32[]{:S(2)}) async-start(), calls=%async_computation.25 | async-start | bytes 974848 | tf_op jit(solution)/shard_map/reduce_scatter | solution.py:63
  1549.4 107.1 %copy-start.17 = (bf16[128,112]{0,1:T(8,128)(2,1)S(1)}, bf16[128,112]{0,1:T(8,128)(2,1)}, u32[]{:S(2)}) copy-start(bf16[128,112]{0,1:T(8,128)(2,1)} %copy-done.16) | copy-start | bytes 86020
  (25 other events, 19.9 us)
Sparse Core Ops, SparseCore 0:
  32.4 110.2 all-reduce.12
  157.1 78.9 reduce-scatter.37
  256.9 108.9 all-reduce.14
  376.4 79.0 reduce-scatter.39
  476.6 107.7 all-reduce.16
  592.2 79.0 reduce-scatter.41
  691.9 106.8 all-reduce.18
  803.9 79.1 reduce-scatter.43
  904.0 55.1 reduce-scatter.27
  979.1 107.6 all-reduce.20
  1089.4 58.3 reduce-scatter.29
  1167.8 107.7 all-reduce.22
  1278.9 58.3 reduce-scatter.31
  1358.6 107.8 all-reduce.24
  1468.9 58.4 reduce-scatter.33
  1548.6 107.8 all-reduce.26
  1659.4 58.5 reduce-scatter.35
